TPU v7x, 32 devices: a whole 2x2x4 slice. The times are simulated.
32 devices in a mesh: vec: 4 (over y, x), orb: 8 (over z, core).
Axes of the slice: x: 2, y: 2, z: 4, core: 2. Of those that a mesh axis runs over, the one named last changes fastest.
Arguments:
- chol_occ: float32 [44, 96, 1056], P('vec', 'orb'), may hold values from -6 to 6
- chol_vir: float32 [44, 960, 1056], P('vec', 'orb'), may hold values from -6 to 6
- singles: float32 [96, 960], P('orb'), may hold values from -0.6 to 0.6
Outputs:
- dressed_vir: float32 [44, 960, 1056], P('vec', 'orb')
- dressed_ov: float32 [44, 96, 960], P(None, 'orb', 'vec')
- fock_ov: float32 [96, 960], P('orb')
All inputs are finite; a program needn't handle non-finite values.
Results may differ from a plain program's by a relative error of at most 0.000086.
Values sent between devices are 32-bit elements; how exact they have to be, the bound alone decides.
A program may use at most 64 MiB of HBM per device.

v0:
```python
import jax
import jax.numpy as jnp
from jax import lax
from jax.sharding import PartitionSpec as P


def dress_right(matrix_rows, amplitudes):
    occ_width = amplitudes.shape[0]
    occ_cols = matrix_rows[:, :, :occ_width]
    extra_term = jnp.einsum("qrj,ja->qra", occ_cols, amplitudes, precision=lax.Precision.HIGHEST)
    return jnp.concatenate([occ_cols, matrix_rows[:, :, occ_width:] + extra_term], axis=2)


def dress_left(vir_rows, occ_all, amp_cols):
    return vir_rows - jnp.einsum("qin,ia->qan", occ_all, amp_cols, precision=lax.Precision.HIGHEST)


def shards(chol_occ, chol_vir, singles):
    amplitudes = lax.all_gather(singles, "orb", axis=0, tiled=True)
    occ_width = amplitudes.shape[0]
    vir_local = chol_vir.shape[1]
    vir_start = lax.axis_index("orb") * vir_local
    amp_cols = lax.dynamic_slice_in_dim(amplitudes, vir_start, vir_local, 1)
    occ_all = lax.all_gather(chol_occ, "orb", axis=1, tiled=True)
    dressed_vir = dress_right(dress_left(chol_vir, occ_all, amp_cols), amplitudes)
    dressed_occ = dress_right(chol_occ, amplitudes)
    local_rows = chol_occ.shape[1]
    first_row = lax.axis_index("orb") * local_rows
    row_ids = lax.broadcasted_iota(jnp.int32, (local_rows, chol_occ.shape[2]), 0) + first_row
    col_ids = lax.broadcasted_iota(jnp.int32, (local_rows, chol_occ.shape[2]), 1)
    diag_mask = jnp.where(row_ids == col_ids, 1.0, 0.0).astype(jnp.float32)
    traces_local = jnp.sum(chol_occ * diag_mask[None], axis=(1, 2))
    traces = lax.psum(traces_local, "orb")
    ov_block = dressed_occ[:, :, occ_width:]
    total_vectors = chol_occ.shape[0] * lax.axis_size("vec")
    fock_part = (
        jnp.einsum("q,qia->ia", traces, ov_block, precision=lax.Precision.HIGHEST) / total_vectors
    )
    fock_ov = lax.psum(fock_part, "vec")
    pair_blocks = lax.all_to_all(ov_block, "vec", split_axis=2, concat_axis=0, tiled=True)
    return (dressed_vir, pair_blocks, fock_ov)


def solution(mesh):
    return jax.shard_map(
        shards,
        mesh=mesh,
        in_specs=(P("vec", "orb", None), P("vec", "orb", None), P("orb", None)),
        out_specs=(P("vec", "orb", None), P(None, "orb", "vec"), P("orb", None)),
        check_vma=False,
    )
```

profile of v0, /device:TPU:0, one launch (start us, length us, event | category | flops | bytes accessed | tf_op | source)
XLA Modules:
  0.0 127.6 jit_solution(5254257879419233849)
XLA Ops:
  7.2 0.0 all-gather.3.cloned.1.call-start
  7.2 2.3 %copy.10 = f32[11,12,1056]{2,0,1:T(8,128)} copy(f32[11,12,1056]{2,1,0:T(8,128)} %param.3) | data formatting | bytes 1115136 | tf_op args[0]
  9.5 0.0 all-gather.3.cloned.1.call-update
  9.5 16.7 %all-gather = f32[8,12,960]{2,1,0:T(8,128)S(1)} all-gather(f32[1,12,960]{2,1,0:T(8,128)} %bitcast.22), channel_id=1, replica_groups=mesh['vec'=4,'orb'=8] {'orb'}, dimensions={0}, use_global_device_ids=true | all-gather | bytes 414720 | tf_op jit(solution)/shard_map/all_gather | solution.py:19
  26.3 1.9 %convolution_add_fusion = f32[11,12,960]{2,1,0:T(8,128)S(1)} fusion(f32[96,960,1]{1,0,2:T(8,128)S(1)} %reshape.23, f32[11,12,1056]{2,1,0:T(8,128)} %param.3), kind=kOutput, calls=%fused_computation.4 | convolution fusion | flops 146108160 | bytes 1433088 | tf_op jit(solution)/shard_map/qrj,ja->qra/dot_general | solution.py:10
  28.2 6.0 %copy.13 = f32[11,12,960]{1,0,2:T(8,128)} copy(f32[11,12,960]{2,1,0:T(8,128)S(1)} %convolution_add_fusion) | data formatting | bytes 1013760 | tf_op jit(solution)/shard_map/add | solution.py:11
  34.2 0.0 copy-start
  34.2 6.5 %reshape.27 = f32[4,1,31680]{2,1,0:T(1,128)} reshape(f32[960,11,12]{2,1,0:T(8,128)} %bitcast.20) | data formatting | bytes 1013760
  40.7 0.1 fusion.4
  40.8 0.0 copy-done
  40.8 0.2 multiply_reduce_fusion
  41.0 3.7 %all-to-all-start = ((f32[4,1,31680]{2,1,0:T(1,128)}), f32[4,1,31680]{2,1,0:T(1,128)S(1)}, u32[]{:S(2)}, u32[]{:S(2)}) async-start(f32[4,1,31680]{2,1,0:T(1,128)} %reshape.27), calls=%async_computation | async-start | bytes 1015808 | tf_op jit(solution)/shard_map/all_to_all | solution.py:40
  44.7 19.3 %psum.14 = f32[11]{0:T(128)S(1)} all-reduce(f32[11]{0:T(128)S(1)} %multiply_reduce_fusion), channel_id=1, replica_groups=mesh['vec'=4,'orb'=8] {'orb'}, use_global_device_ids=true, to_apply=%region_1.2 | all-reduce | flops 11 | bytes 88 | tf_op jit(solution)/shard_map/psum | solution.py:33
  64.0 0.8 fusion.1
  64.9 17.7 %psum.15 = f32[12,960]{1,0:T(8,128)} all-reduce(f32[12,960]{1,0:T(8,128)S(1)} %bitcast_multiply_fusion), channel_id=1, replica_groups=mesh['vec'=4,'orb'=8] {'vec'}, use_global_device_ids=true, to_apply=%region_2.3 | all-reduce | flops 11520 | bytes 92160 | tf_op jit(solution)/shard_map/psum | solution.py:39
  82.5 0.0 all-to-all-done
  82.5 0.5 broadcast.18
  83.0 2.1 %reduce = f32[4,31680]{1,0:T(4,128)S(1)} reduce(f32[4,1,31680]{2,1,0:T(1,128)S(1)} %all-to-all-done, f32[]{:T(128)} %broadcast.18), dimensions={1}, to_apply=%all_to_all.13.reduce_sub_computation | reduce | bytes 1013764 | tf_op jit(solution)/shard_map/all_to_all | solution.py:40
  85.2 6.0 %reshape.28 = f32[960,11,12]{2,1,0:T(8,128)} reshape(f32[4,31680]{1,0:T(4,128)S(1)} %reduce) | data formatting | bytes 1013760
  91.2 6.2 %copy.14 = f32[11,12,4,240]{3,0,2,1:T(8,128)S(1)} copy(f32[11,12,4,240]{1,0,3,2:T(8,128)} %bitcast.19) | data formatting | bytes 1013760 | tf_op jit(solution)/shard_map/all_to_all | solution.py:40
  97.4 0.9 all_to_all.16
  98.3 0.0 all-gather.3.cloned.1.call-done
  98.3 14.5 %bitcast_subtract_fusion = f32[11,120,1056]{1,2,0:T(8,128)S(1)} fusion(f32[11,120,1056]{1,2,0:T(8,128)} %param.4, f32[11,96,1056]{2,0,1:T(8,128)} %all-gather.3.cloned.1.call-done, f32[96,960]{1,0:T(8,128)S(1)} %reshape.21, s32[]{:T(128)S(6)} %select_n.11), kind=kOutput, calls=%fused_computation.1 | convolution fusion | flops 1607189760 | bytes 15661060 | tf_op jit(solution)/shard_map/qin,ia->qan/dot_general | solution.py:15
  112.9 4.7 %slice_add_fusion = f32[11,120,960]{1,2,0:T(8,128)S(1)} fusion(f32[11,120,1056]{1,2,0:T(8,128)S(1)} %bitcast_subtract_fusion, f32[96,960,1]{1,0,2:T(8,128)S(1)} %reshape.23), kind=kOutput, calls=%fused_computation.2 | convolution fusion | flops 1461081600 | bytes 11013120 | tf_op jit(solution)/shard_map/qrj,ja->qra/dot_general | solution.py:10
  117.6 3.2 %pad_maximum_fusion = f32[11,120,1056]{1,2,0:T(8,128)} fusion(f32[11,120,960]{1,2,0:T(8,128)S(1)} %slice_add_fusion, f32[11,120,96]{1,2,0:T(8,128)S(1)} %slice.16), kind=kLoop, calls=%fused_computation | loop fusion | flops 1393920 | bytes 11151360 | tf_op jit(solution)/shard_map/concatenate | solution.py:11
  (5 shorter events, 0.1 us)
Async XLA Ops:
  7.2 91.1 %all-gather.3.cloned.1.call-start = ((), (), s32[]{:S(2)}) async-start(), calls=%async_computation.1 | async-start | bytes 7962624 | tf_op jit(solution)/shard_map/all_gather | solution.py:24
  34.2 6.6 %copy-start = (f32[11,12,1056]{2,1,0:T(8,128)S(1)}, f32[11,12,1056]{2,1,0:T(8,128)}, u32[]{:S(2)}) copy-start(f32[11,12,1056]{2,1,0:T(8,128)} %param.3) | copy-start | bytes 1672708
  41.0 41.6 %all-to-all-start = ((f32[4,1,31680]{2,1,0:T(1,128)}), f32[4,1,31680]{2,1,0:T(1,128)S(1)}, u32[]{:S(2)}, u32[]{:S(2)}) async-start(f32[4,1,31680]{2,1,0:T(1,128)} %reshape.27), calls=%async_computation | async-start | bytes 1015808 | tf_op jit(solution)/shard_map/all_to_all | solution.py:40
Sparse Core Ops, SparseCore 0:
  10.2 74.4 all-gather.2
where the time goes:
time: 128 us
  blocking collectives  53.7 us (42%)
  local copies, waits for them, and re-layouts  28.5 us (22%)
  matrix products  22 us (17%)
  between operations  14.1 us (11%)
  other arithmetic  5.58 us (4%)
  starting transfers between devices  3.76 us (3%)
    psum x1, blocking collectives, shards(): traces = lax.psum(traces_local, 'orb')  19.3 us
    psum x1, blocking collectives, shards(): fock_ov = lax.psum(fock_part, 'vec')  17.7 us
    all_gather x1, blocking collectives, shards(): amplitudes = lax.all_gather(singles, 'orb', axis=0, tiled=True)  16.7 us
    unnamed x7, local copies, waits for them, and re-layouts  14.9 us
    dot_general x1, matrix products, dress_left(): jnp.einsum('qin,ia->qan', occ_all, amp_cols, precision=lax.Precision.HIGH...  14.5 us
    all_to_all x3, local copies, waits for them, and re-layouts, shards(): lax.all_to_all(ov_block, 'vec', split_axis=2, concat_axis=0, tiled=True)  7.57 us
    dot_general x2, matrix products, dress_right(): jnp.einsum('qrj,ja->qra', occ_cols, amplitudes, precision=lax.Precision.H...  6.66 us
    add x1, local copies, waits for them, and re-layouts, dress_right(): matrix_rows[:, :, occ_width:] + extra_term  5.96 us
  transfers between devices with their start and end apart: 2, of which 0 were waited for; matrix products, arithmetic and copies ran while one was open for 24% of the time, Pallas kernels for 0%

commit v1 on v0

--- a/solution.py
+++ b/solution.py
@@ -36,7 +36,9 @@
     fock_part = (
         jnp.einsum("q,qia->ia", traces, ov_block, precision=lax.Precision.HIGHEST) / total_vectors
     )
-    fock_ov = lax.psum(fock_part, "vec")
+    fock_ov = fock_part
+    for hop in (1, 2):
+        fock_ov = fock_ov + lax.ppermute(fock_ov, "vec", [(dev, dev ^ hop) for dev in range(4)])
     pair_blocks = lax.all_to_all(ov_block, "vec", split_axis=2, concat_axis=0, tiled=True)
     return (dressed_vir, pair_blocks, fock_ov)
 

time: 128 us -> 120 us (0.938)
  blocking collectives: 53.7 us -> 36.2 us
  waiting for transfers between devices: 0.02 us -> 5.16 us
  starting transfers between devices: 3.76 us -> 7.24 us
    psum x1 -> x0, blocking collectives: 17.7 us -> none  [shards(): fock_ov = lax.psum(fock_part, 'vec')]
    ppermute x0 -> x2, waiting for transfers between devices: none -> 5.14 us  [shards(): lax.ppermute(fock_ov, 'vec', [(dev, dev ^ hop) for dev in range(4)])]
    ppermute x0 -> x2, starting transfers between devices: none -> 3.48 us  [shards(): lax.ppermute(fock_ov, 'vec', [(dev, dev ^ hop) for dev in range(4)])]
  transfers between devices with their start and end apart: 2 -> 4, of which waited for: 0 -> 2; matrix products, arithmetic and copies ran while one was open for 24% -> 26% of each run, Pallas kernels for 0% -> 0%
where the time goes in v1:
time: 120 us; the launch traced here: 119 us
  blocking collectives  36.2 us (30%)
  local copies, waits for them, and re-layouts  28.5 us (24%)
  matrix products  22 us (18%)
  between operations  14.1 us (12%)
  starting transfers between devices  7.24 us (6%)
  other arithmetic  6.23 us (5%)
  waiting for transfers between devices  5.16 us (4%)
    psum x1, blocking collectives, shards(): traces = lax.psum(traces_local, 'orb')  19.5 us
    all_gather x1, blocking collectives, shards(): amplitudes = lax.all_gather(singles, 'orb', axis=0, tiled=True)  16.7 us
    unnamed x7, local copies, waits for them, and re-layouts  14.9 us
    dot_general x1, matrix products, dress_left(): jnp.einsum('qin,ia->qan', occ_all, amp_cols, precision=lax.Precision.HIGH...  14.5 us
    all_to_all x3, local copies, waits for them, and re-layouts, shards(): lax.all_to_all(ov_block, 'vec', split_axis=2, concat_axis=0, tiled=True)  7.6 us
    dot_general x2, matrix products, dress_right(): jnp.einsum('qrj,ja->qra', occ_cols, amplitudes, precision=lax.Precision.H...  6.66 us
    add x1, local copies, waits for them, and re-layouts, dress_right(): matrix_rows[:, :, occ_width:] + extra_term  5.96 us
    ppermute x2, waiting for transfers between devices, shards(): lax.ppermute(fock_ov, 'vec', [(dev, dev ^ hop) for dev in range(4)])  5.14 us
  transfers between devices with their start and end apart: 4, of which 2 were waited for; matrix products, arithmetic and copies ran while one was open for 26% of the time, Pallas kernels for 0%

profile of v1, /device:TPU:0, one launch (start us, length us, event | category | flops | bytes accessed | tf_op | source)
XLA Modules:
  0.0 119.5 jit_solution(11190042272631445356)
XLA Ops:
  7.2 0.0 all-gather.3.cloned.1.call-start
  7.2 2.3 %copy.10 = f32[11,12,1056]{2,0,1:T(8,128)} copy(f32[11,12,1056]{2,1,0:T(8,128)} %param.3) | data formatting | bytes 1115136 | tf_op args[0]
  9.5 0.0 all-gather.3.cloned.1.call-update
  9.5 16.7 %all-gather = f32[8,12,960]{2,1,0:T(8,128)S(1)} all-gather(f32[1,12,960]{2,1,0:T(8,128)} %bitcast.24), channel_id=1, replica_groups=mesh['vec'=4,'orb'=8] {'orb'}, dimensions={0}, use_global_device_ids=true | all-gather | bytes 414720 | tf_op jit(solution)/shard_map/all_gather | solution.py:19
  26.3 1.9 %convolution_add_fusion = f32[11,12,960]{2,1,0:T(8,128)S(1)} fusion(f32[96,960,1]{1,0,2:T(8,128)S(1)} %reshape.23, f32[11,12,1056]{2,1,0:T(8,128)} %param.3), kind=kOutput, calls=%fused_computation.4 | convolution fusion | flops 146108160 | bytes 1433088 | tf_op jit(solution)/shard_map/qrj,ja->qra/dot_general | solution.py:10
  28.2 6.0 %copy.13 = f32[11,12,960]{1,0,2:T(8,128)} copy(f32[11,12,960]{2,1,0:T(8,128)S(1)} %convolution_add_fusion) | data formatting | bytes 1013760 | tf_op jit(solution)/shard_map/add | solution.py:11
  34.2 0.0 copy-start
  34.2 6.5 %reshape.27 = f32[4,1,31680]{2,1,0:T(1,128)} reshape(f32[960,11,12]{2,1,0:T(8,128)} %bitcast.22) | data formatting | bytes 1013760
  40.7 0.1 fusion.4
  40.8 0.0 copy-done
  40.8 0.2 multiply_reduce_fusion
  41.0 3.7 %all-to-all-start = ((f32[4,1,31680]{2,1,0:T(1,128)}), f32[4,1,31680]{2,1,0:T(1,128)S(1)}, u32[]{:S(2)}, u32[]{:S(2)}) async-start(f32[4,1,31680]{2,1,0:T(1,128)} %reshape.27), calls=%async_computation | async-start | bytes 1015808 | tf_op jit(solution)/shard_map/all_to_all | solution.py:42
  44.7 19.5 %psum.7 = f32[11]{0:T(128)S(1)} all-reduce(f32[11]{0:T(128)S(1)} %multiply_reduce_fusion), channel_id=1, replica_groups=mesh['vec'=4,'orb'=8] {'orb'}, use_global_device_ids=true, to_apply=%region_1.2 | all-reduce | flops 11 | bytes 88 | tf_op jit(solution)/shard_map/psum | solution.py:33
  64.2 0.8 fusion.1
  65.0 1.7 %collective-permute-start = (f32[12,960]{1,0:T(8,128)S(1)}, f32[12,960]{1,0:T(8,128)S(1)}, u32[]{:S(2)}, u32[]{:S(2)}) collective-permute-start(f32[12,960]{1,0:T(8,128)S(1)} %bitcast_multiply_fusion), channel_id=1, source_target_pairs={{0,8},{8,0},{16,24},{24,16},{1,9},{9,1},{17,25},{25,17},{2,10},{10... | collective-permute-start | bytes 138248 | tf_op jit(solution)/shard_map/ppermute | solution.py:41
  66.8 2.6 %collective-permute-done = f32[12,960]{1,0:T(8,128)S(1)} collective-permute-done((f32[12,960]{1,0:T(8,128)S(1)}, f32[12,960]{1,0:T(8,128)S(1)}, u32[]{:S(2)}, u32[]{:S(2)}) %collective-permute-start) | collective-permute-done | bytes 46112 | tf_op jit(solution)/shard_map/ppermute | solution.py:41
  69.4 1.7 %collective-permute-start.1 = (f32[12,960]{1,0:T(8,128)S(1)}, f32[12,960]{1,0:T(8,128)S(1)}, u32[]{:S(2)}, u32[]{:S(2)}) collective-permute-start(f32[12,960]{1,0:T(8,128)S(1)} %fusion.8), channel_id=1, source_target_pairs={{0,16},{8,24},{16,0},{24,8},{1,17},{9,25},{17,1},{25,9},{2,18},{10... | collective-permute-start | bytes 138248 | tf_op jit(solution)/shard_map/ppermute | solution.py:41
  71.2 2.5 %collective-permute-done.1 = f32[12,960]{1,0:T(8,128)S(1)} collective-permute-done((f32[12,960]{1,0:T(8,128)S(1)}, f32[12,960]{1,0:T(8,128)S(1)}, u32[]{:S(2)}, u32[]{:S(2)}) %collective-permute-start.1) | collective-permute-done | bytes 46112 | tf_op jit(solution)/shard_map/ppermute | solution.py:41
  73.7 0.6 add.30
  74.3 0.0 all-to-all-done
  74.3 0.5 broadcast.18
  74.9 2.1 %reduce = f32[4,31680]{1,0:T(4,128)S(1)} reduce(f32[4,1,31680]{2,1,0:T(1,128)S(1)} %all-to-all-done, f32[]{:T(128)} %broadcast.18), dimensions={1}, to_apply=%all_to_all.13.reduce_sub_computation | reduce | bytes 1013764 | tf_op jit(solution)/shard_map/all_to_all | solution.py:42
  77.0 6.0 %reshape.28 = f32[960,11,12]{2,1,0:T(8,128)} reshape(f32[4,31680]{1,0:T(4,128)S(1)} %reduce) | data formatting | bytes 1013760
  83.0 6.2 %copy.14 = f32[11,12,4,240]{3,0,2,1:T(8,128)S(1)} copy(f32[11,12,4,240]{1,0,3,2:T(8,128)} %bitcast.21) | data formatting | bytes 1013760 | tf_op jit(solution)/shard_map/all_to_all | solution.py:42
  89.2 0.9 all_to_all.16
  90.1 0.0 all-gather.3.cloned.1.call-done
  90.1 14.5 %bitcast_subtract_fusion = f32[11,120,1056]{1,2,0:T(8,128)S(1)} fusion(f32[11,120,1056]{1,2,0:T(8,128)} %param.4, f32[11,96,1056]{2,0,1:T(8,128)} %all-gather.3.cloned.1.call-done, f32[96,960]{1,0:T(8,128)S(1)} %reshape.21, s32[]{:T(128)S(6)} %select_n.11), kind=kOutput, calls=%fused_computation.1 | convolution fusion | flops 1607189760 | bytes 15661060 | tf_op jit(solution)/shard_map/qin,ia->qan/dot_general | solution.py:15
  104.7 4.7 %slice_add_fusion = f32[11,120,960]{1,2,0:T(8,128)S(1)} fusion(f32[11,120,1056]{1,2,0:T(8,128)S(1)} %bitcast_subtract_fusion, f32[96,960,1]{1,0,2:T(8,128)S(1)} %reshape.23), kind=kOutput, calls=%fused_computation.2 | convolution fusion | flops 1461081600 | bytes 11013120 | tf_op jit(solution)/shard_map/qrj,ja->qra/dot_general | solution.py:10
  109.5 3.2 %pad_maximum_fusion = f32[11,120,1056]{1,2,0:T(8,128)} fusion(f32[11,120,960]{1,2,0:T(8,128)S(1)} %slice_add_fusion, f32[11,120,96]{1,2,0:T(8,128)S(1)} %slice.16), kind=kLoop, calls=%fused_computation | loop fusion | flops 1393920 | bytes 11151360 | tf_op jit(solution)/shard_map/concatenate | solution.py:11
  (6 shorter events, 0.2 us)
Async XLA Ops:
  7.2 83.0 %all-gather.3.cloned.1.call-start = ((), (), s32[]{:S(2)}) async-start(), calls=%async_computation.1 | async-start | bytes 7962624 | tf_op jit(solution)/shard_map/all_gather | solution.py:24
  34.2 6.6 %copy-start = (f32[11,12,1056]{2,1,0:T(8,128)S(1)}, f32[11,12,1056]{2,1,0:T(8,128)}, u32[]{:S(2)}) copy-start(f32[11,12,1056]{2,1,0:T(8,128)} %param.3) | copy-start | bytes 1672708
  41.0 33.4 %all-to-all-start = ((f32[4,1,31680]{2,1,0:T(1,128)}), f32[4,1,31680]{2,1,0:T(1,128)S(1)}, u32[]{:S(2)}, u32[]{:S(2)}) async-start(f32[4,1,31680]{2,1,0:T(1,128)} %reshape.27), calls=%async_computation | async-start | bytes 1015808 | tf_op jit(solution)/shard_map/all_to_all | solution.py:42
  65.0 4.3 %collective-permute-start = (f32[12,960]{1,0:T(8,128)S(1)}, f32[12,960]{1,0:T(8,128)S(1)}, u32[]{:S(2)}, u32[]{:S(2)}) collective-permute-start(f32[12,960]{1,0:T(8,128)S(1)} %bitcast_multiply_fusion), channel_id=1, source_target_pairs={{0,8},{8,0},{16,24},{24,16},{1,9},{9,1},{17,25},{25,17},{2,10},{10... | collective-permute-start | bytes 138248 | tf_op jit(solution)/shard_map/ppermute | solution.py:41
  69.4 4.3 %collective-permute-start.1 = (f32[12,960]{1,0:T(8,128)S(1)}, f32[12,960]{1,0:T(8,128)S(1)}, u32[]{:S(2)}, u32[]{:S(2)}) collective-permute-start(f32[12,960]{1,0:T(8,128)S(1)} %fusion.8), channel_id=1, source_target_pairs={{0,16},{8,24},{16,0},{24,8},{1,17},{9,25},{17,1},{25,9},{2,18},{10... | collective-permute-start | bytes 138248 | tf_op jit(solution)/shard_map/ppermute | solution.py:41
Sparse Core Ops, SparseCore 0:
  10.2 74.4 all-gather.2
